TPU v7x, 32 devices: a whole 2x2x4 slice. The times are simulated.
32 devices in a mesh: frames: 4 (over x, core), feat: 8 (over z, y).
Axes of the slice: x: 2, y: 2, z: 4, core: 2. Of those that a mesh axis runs over, the one named last changes fastest.
Arguments:
- acoustic: float32 [1024, 440], P('frames'), may hold values from -6 to 6
- projection: float32 [440, 8192], P(None, 'feat'), may hold values from -0.25 to 0.25
- phases: float32 [8192], P('feat'), may hold values from -3.140625 to 3.140625
- labels: int32 [1024], P('frames'), may hold values from 0 to 146
- weights: float32 [147, 8192], P(None, 'feat'), may hold values from -1.5 to 1.5
- scaled_duals: float32 [147, 1024], P(None, 'frames'), may hold values from -7 to 7
Outputs:
- weights_out: float32 [147, 8192], P(None, 'feat')
- duals_out: float32 [147, 1024], P(None, ('frames', 'feat'))
- penalty: float32 [], replicated
All inputs are finite; a program needn't handle non-finite values.
Results may differ from a plain program's by a relative error of at most 0.0003.
Values sent between devices are 32-bit elements; how exact they have to be, the bound alone decides.
No kernel may reach another device: no remote copies, remote signals or barrier semaphores. Data moves between devices by JAX's collectives and lax.ppermute only.
A program may use at most 64 MiB of HBM per device.

v0:
```python
import jax
import jax.numpy as jnp
from jax import lax
from jax.sharding import PartitionSpec as P

ITERS = 2
highest = lax.Precision.HIGHEST
epsilon = 1e-06
ridge_weight = 2.0


def cosine_features(acoustic, projection, phases, total_features):
    mixed = (
        jnp.dot(acoustic, projection, precision=highest, preferred_element_type=jnp.float32)
        + phases[None, :]
    )
    return jnp.sqrt(2.0 / total_features) * jnp.cos(mixed)


def ridge_solve(factor, right):
    middle = lax.linalg.triangular_solve(
        factor, right, left_side=False, lower=True, transpose_a=True
    )
    return lax.linalg.triangular_solve(
        factor, middle, left_side=False, lower=True, transpose_a=False
    )


def proximal(predicted, duals, target, penalty):
    shifted = predicted + duals
    inner = (2.0 * target + penalty * shifted) / (2.0 + penalty)
    split = jnp.where(target * shifted < 1.0, inner, shifted)
    miss = predicted - split
    duals_next = duals + miss
    residual = split - duals_next - predicted
    return (miss, duals_next, residual)


def shards(acoustic, projection, phases, labels, weights, scaled_duals):
    frames_here = acoustic.shape[0]
    block_width = projection.shape[1]
    class_count = weights.shape[0]
    feat_count = lax.axis_size("feat")
    group_count = lax.axis_size("frames")
    total_features = block_width * feat_count
    total_frames = frames_here * group_count
    ridge = frames_here / total_features
    share = frames_here // feat_count
    offset = lax.axis_index("feat") * share
    basis = cosine_features(acoustic, projection, phases, total_features)
    inner_matrix = ridge * jnp.eye(frames_here, dtype=jnp.float32) + lax.dot_general(
        basis, basis, (((1,), (1,)), ((), ())), precision=highest
    )
    factor = jnp.linalg.cholesky(inner_matrix)
    classes = lax.broadcasted_iota(jnp.int32, (class_count, frames_here), 0)
    target = jnp.where(classes == labels[None, :], 1.0, -1.0).astype(jnp.float32)
    duals = scaled_duals
    penalty = jnp.ones((), jnp.float32)
    for iteration in range(ITERS):
        partial_value = lax.dot_general(weights, basis, (((1,), (1,)), ((), ())), precision=highest)
        predicted = lax.psum(partial_value, "feat")
        miss, duals, residual = proximal(predicted, duals, target, penalty)
        mine = lax.dynamic_slice_in_dim(miss, offset, share, 1)
        primal_part = jnp.sum(mine * mine)
        proj = (
            jnp.dot(residual, basis, precision=highest, preferred_element_type=jnp.float32)
            / feat_count
        )
        coef = lax.dot_general(proj, basis, (((1,), (1,)), ((), ())), precision=highest)
        solved = ridge_solve(factor, coef)
        back = jnp.dot(solved, basis, precision=highest, preferred_element_type=jnp.float32)
        local = weights + (proj - back) / ridge
        summed, primal_groups = lax.psum((local, primal_part), "frames")
        updated = penalty / (ridge_weight + penalty * group_count) * summed
        moved = updated - weights
        change, primal = lax.psum((jnp.sum(moved * moved), primal_groups), "feat")
        ratio = (primal / (total_frames * class_count) + epsilon) / (
            group_count * penalty * penalty * change / (total_features * class_count) + epsilon
        )
        next_penalty = penalty * jnp.sqrt(jnp.sqrt(ratio))
        duals = duals * (penalty / next_penalty)
        penalty = next_penalty
        weights = updated
    duals = lax.dynamic_slice_in_dim(duals, offset, share, 1)
    return (weights, duals, penalty)


def solution(mesh):
    return jax.shard_map(
        shards,
        mesh=mesh,
        in_specs=(
            P("frames", None),
            P(None, "feat"),
            P("feat"),
            P("frames"),
            P(None, "feat"),
            P(None, "frames"),
        ),
        out_specs=(P(None, "feat"), P(None, ("frames", "feat")), P()),
        check_vma=False,
    )
```

profile of v0, /device:TPU:0, one launch (start us, length us, event | category | flops | bytes accessed | tf_op | source)
XLA Modules:
  0.0 297.5 jit_solution(15187236382029461404)
XLA Ops:
  7.2 0.0 all-reduce.8.cloned.1.call-start
  7.2 1.4 copy-done
  8.7 13.2 %fusion.1 = f32[256,1024]{1,0:T(8,128)S(1)} fusion(f32[256,440]{0,1:T(8,128)} %param.10, f32[440,1024]{1,0:T(8,128)S(1)} %copy-done, f32[1024]{0:T(1024)} %param.12), kind=kOutput, calls=%fused_computation.4 | convolution fusion | flops 1384644608 | bytes 3305472 | tf_op jit(solution)/shard_map/dot_general | solution.py:14
  21.8 1.9 convolution_bitcast_fusion
  23.7 0.0 all-reduce.8.cloned.1.call-update
  23.7 0.2 all-reduce.10.cloned.1.call-start
  24.0 1.7 fusion.69
  25.7 1.8 copy.9
  27.5 1.1 fusion.10
  28.6 0.7 copy-done.8
  29.3 0.6 cholesky.115
  29.9 12.5 %cholesky.49 = f32[128,128]{1,0:T(8,128)S(1)} custom-call(f32[128,128]{1,0:T(8,128)} %cholesky.115), custom_call_target="Cholesky" | custom-call | tf_op jit(solution)/shard_map/jit(cholesky)/cholesky | solution.py:54
  42.5 0.6 select_reduce_fusion.1
  43.1 11.3 %custom-call.17 = f32[1,128,128]{1,2,0:T(8,128)} custom-call(f32[1,128,128]{2,1,0:T(8,128)} %get-tuple-element.63), custom_call_target="InvertDiagBlocksLowerTriangular" | custom-call | tf_op jit(solution)/shard_map/jit(cholesky)/cholesky | solution.py:54
  54.4 0.7 cholesky.111
  55.1 1.7 constant_dynamic-update-slice_fusion
  56.8 1.7 convolution_subtract_fusion.6
  58.5 12.5 %cholesky.103 = f32[128,128]{1,0:T(8,128)S(1)} custom-call(f32[128,128]{1,0:T(8,128)} %convolution_subtract_fusion.6), custom_call_target="Cholesky" | custom-call | tf_op jit(solution)/shard_map/jit(cholesky)/cholesky | solution.py:54
  71.1 0.6 select_reduce_fusion
  71.7 0.7 compare_reduce_fusion
  73.8 1.7 select_select_fusion
  75.5 0.1 broadcast.169
  75.5 7.0 %while.8 = (s32[]{:T(128)}, f32[256,256]{1,0:T(8,128)}, s32[2,2]{1,0:T(2,128)S(1)}, f32[2,128,128]{2,1,0:T(8,128)}, s32[]{:T(128)}) while((s32[]{:T(128)}, f32[256,256]{1,0:T(8,128)}, s32[2,2]{1,0:T(2,128)S(1)}, f32[2,128,128]{2,1,0:T(8,128)}, s32[]{:T(128)}) %tuple.44), condition=%wide.while_cond, body=%wide.while_body.sunk | while | flops 2 | bytes 132205 | solution.py:21
  75.5 0.6 fusion.100
  76.1 2.9 bitcast_dynamic-update-slice_fusion.2
  79.1 0.6 fusion.100
  79.6 2.9 bitcast_dynamic-update-slice_fusion.2
  82.5 21.1 %custom-call.20 = f32[2,128,128]{1,2,0:T(8,128)} custom-call(f32[2,128,128]{2,1,0:T(8,128)} %get-tuple-element.33), custom_call_target="InvertDiagBlocksLowerTriangular" | custom-call | tf_op jit(solution)/shard_map/triangular_solve/custom-call.0 | solution.py:21
  103.6 1.7 fusion.66
  105.3 1.9 convolution_multiply_fusion.1
  107.2 1.2 fusion.70
  108.5 0.3 fusion.33
  108.8 0.3 convolution_subtract_fusion.5
  109.1 0.3 fusion.47
  109.3 0.3 fusion.48
  109.6 0.3 convolution_subtract_fusion.4
  109.9 0.3 fusion.44
  110.2 1.6 fusion.3
  111.9 0.0 all-reduce.12.cloned.1.call-start
  111.9 1.6 multiply_reduce_fusion.3
  113.5 9.0 %psum.71 = f32[]{:T(128)} all-reduce(f32[]{:T(128)} %multiply_reduce_fusion.3), channel_id=1, replica_groups=mesh['frames'=4,'feat'=8] {'frames'}, use_global_device_ids=true, to_apply=%region_2.3 | all-reduce | flops 1 | bytes 8 | tf_op jit(solution)/shard_map/psum | solution.py:73
  122.5 26.2 %all-reduce.10.cloned.1.call-done = f32[147,1024]{1,0:T(8,128)} async-done(((f32[147,1024]{1,0:T(8,128)}), f32[147,1024]{1,0:T(8,128)}) %all-reduce.10.cloned.1.call-update) | async-done | bytes 602128 | tf_op jit(solution)/shard_map/psum | solution.py:73
  148.7 3.0 %fusion.6 = f32[147,256]{1,0:T(8,128)} fusion(f32[256,1024]{1,0:T(8,128)S(1)} %fusion.1, f32[147,1024]{1,0:T(8,128)} %all-reduce.10.cloned.1.call-done), kind=kOutput, calls=%fused_computation.21 | convolution fusion | flops 462572544 | bytes 1801216 | tf_op jit(solution)/shard_map/dot_general | solution.py:60
  151.7 0.0 all-reduce.14.cloned.1.call-start
  151.8 1.8 multiply_reduce_fusion.1
  153.6 22.0 %all-reduce.2 = (f32[]{:T(128)}, f32[]{:T(128)}) all-reduce(f32[]{:T(128)} %psum.71, f32[]{:T(128)} %multiply_reduce_fusion.1), channel_id=1, replica_groups=mesh['frames'=4,'feat'=8] {'feat'}, use_global_device_ids=true, to_apply=%region_3.4 | all-reduce | flops 2 | bytes 16 | tf_op jit(solution)/shard_map/psum | solution.py:76
  177.1 45.5 %all-reduce.12.cloned.1.call-done = f32[147,256]{1,0:T(8,128)} async-done(((f32[147,256]{1,0:T(8,128)}), f32[147,256]{1,0:T(8,128)}) %all-reduce.12.cloned.1.call-update) | async-done | bytes 150544 | tf_op jit(solution)/shard_map/psum | solution.py:61
  222.6 1.9 convolution_multiply_fusion
  224.4 1.2 fusion.71
  225.7 0.3 fusion.31
  226.0 0.3 convolution_subtract_fusion.3
  226.3 0.3 fusion.45
  226.6 0.3 fusion.46
  226.9 0.3 convolution_subtract_fusion.2
  227.1 0.3 fusion.43
  227.4 1.6 fusion.5
  229.1 1.1 fusion.54
  230.2 0.7 multiply_reduce_fusion.2
  230.9 6.3 %psum.77 = f32[]{:T(128)} all-reduce(f32[]{:T(128)} %multiply_reduce_fusion.2), channel_id=1, replica_groups=mesh['frames'=4,'feat'=8] {'frames'}, use_global_device_ids=true, to_apply=%region_14.17 | all-reduce | flops 1 | bytes 8 | tf_op jit(solution)/shard_map/psum | solution.py:73
  237.2 25.8 %all-reduce.14.cloned.1.call-done = f32[147,1024]{1,0:T(8,128)} async-done(((f32[147,1024]{1,0:T(8,128)}), f32[147,1024]{1,0:T(8,128)}) %all-reduce.14.cloned.1.call-update) | async-done | bytes 602128 | tf_op jit(solution)/shard_map/psum | solution.py:73
  263.0 2.6 multiply_reduce_fusion
  265.6 22.0 %all-reduce.1 = (f32[]{:T(128)}, f32[]{:T(128)}) all-reduce(f32[]{:T(128)} %psum.77, f32[]{:T(128)} %get-tuple-element.52), channel_id=1, replica_groups=mesh['frames'=4,'feat'=8] {'feat'}, use_global_device_ids=true, to_apply=%region_15.18 | all-reduce | flops 2 | bytes 16 | tf_op jit(solution)/shard_map/psum | solution.py:76
  289.1 0.1 dynamic-slice_multiply_fusion
  289.2 0.7 copy.10
  (26 shorter events, 0.1 us)
Async XLA Ops:
  7.2 1.5 copy-start
  7.2 14.7 %copy-start.2 = (f32[147,1024]{1,0:T(8,128)S(1)}, f32[147,1024]{1,0:T(8,128)}, u32[]{:S(2)}) copy-start(f32[147,1024]{1,0:T(8,128)} %param.14) | copy-start | bytes 1806340
  7.2 96.4 %all-reduce.8.cloned.1.call-start = ((), (), s32[]{:S(2)}) async-start(), calls=%async_computation | async-start | bytes 311296 | tf_op jit(solution)/shard_map/psum | solution.py:61
  23.7 124.9 %all-reduce.10.cloned.1.call-start = ((), (), s32[]{:S(2)}) async-start(), calls=%async_computation.1 | async-start | bytes 1245184 | tf_op jit(solution)/shard_map/psum | solution.py:73
  27.5 76.1 %copy-start.9 = (s32[256]{0:T(256)S(1)}, s32[256]{0:T(256)}, u32[]{:S(2)}) copy-start(s32[256]{0:T(256)} %param.13) | copy-start | bytes 3076
  28.6 0.7 copy-start.8
  105.3 3.1 %copy-start.5 = (f32[147,256]{1,0:T(8,128)}, f32[147,256]{1,0:T(8,128)S(1)}, u32[]{:S(2)}) copy-start(f32[147,256]{1,0:T(8,128)S(1)} %get-tuple-element.54) | copy-start | bytes 451588
  105.3 3.1 %copy-start.6 = (f32[2,128,128]{1,2,0:T(8,128)S(1)}, f32[2,128,128]{1,2,0:T(8,128)}, u32[]{:S(2)}) copy-start(f32[2,128,128]{1,2,0:T(8,128)} %custom-call.20) | copy-start | bytes 393220
  105.3 3.4 %copy-start.3 = (f32[256,256]{1,0:T(8,128)S(1)}, f32[256,256]{1,0:T(8,128)}, u32[]{:S(2)}) copy-start(f32[256,256]{1,0:T(8,128)} %get-tuple-element.117) | copy-start | bytes 786436
  111.9 110.7 %all-reduce.12.cloned.1.call-start = ((), (), s32[]{:S(2)}) async-start(), calls=%async_computation.2 | async-start | bytes 311296 | tf_op jit(solution)/shard_map/psum | solution.py:61
  148.7 3.1 %copy-start.1 = (f32[147,1024]{1,0:T(8,128)S(1)}, f32[147,1024]{1,0:T(8,128)}, u32[]{:S(2)}) copy-start(f32[147,1024]{1,0:T(8,128)} %all-reduce.10.cloned.1.call-done) | copy-start | bytes 1806340
  151.7 111.3 %all-reduce.14.cloned.1.call-start = ((), (), s32[]{:S(2)}) async-start(), calls=%async_computation.3 | async-start | bytes 1245184 | tf_op jit(solution)/shard_map/psum | solution.py:73
  222.6 3.1 %copy-start.7 = (f32[2,128,128]{1,2,0:T(8,128)S(1)}, f32[2,128,128]{1,2,0:T(8,128)}, u32[]{:S(2)}) copy-start(f32[2,128,128]{1,2,0:T(8,128)} %custom-call.20) | copy-start | bytes 393220
  222.6 3.4 %copy-start.4 = (f32[256,256]{1,0:T(8,128)S(1)}, f32[256,256]{1,0:T(8,128)}, u32[]{:S(2)}) copy-start(f32[256,256]{1,0:T(8,128)} %get-tuple-element.117) | copy-start | bytes 786436
Sparse Core Ops, SparseCore 0:
  23.9 73.2 all-reduce.7
  112.0 36.6 all-reduce.9
  152.6 69.9 all-reduce.11
  229.2 33.7 all-reduce.13
where the time goes:
time: 299 us; the launch traced here: 298 us
  waiting for transfers between devices  97.5 us (33%)
  other arithmetic  71.9 us (24%)
  blocking collectives  59.2 us (20%)
  matrix products  36.1 us (12%)
  between operations  19.5 us (7%)
  local copies, waits for them, and re-layouts  13 us (4%)
    psum x2, waiting for transfers between devices, shards(): summed, primal_groups = lax.psum((local, primal_part), 'frames')  51.9 us
    psum x2, waiting for transfers between devices, shards(): predicted = lax.psum(partial_value, 'feat')  45.5 us
    psum x2, blocking collectives, shards(): change, primal = lax.psum((jnp.sum(moved * moved), primal_groups), 'feat')  44 us
    another operation x6, other arithmetic, shards(): factor = jnp.linalg.cholesky(inner_matrix)  38.4 us
    another operation x4, other arithmetic, ridge_solve(): lax.linalg.triangular_solve(factor, right, left_side=False, lower=True, t...  22.8 us
    psum x2, blocking collectives, shards(): summed, primal_groups = lax.psum((local, primal_part), 'frames')  15.3 us
    dot_general x1, matrix products, cosine_features(): jnp.dot(acoustic, projection, precision=highest, preferred_element_type=j...  13.2 us
    another operation x7, local copies, waits for them, and re-layouts, ridge_solve(): lax.linalg.triangular_solve(factor, right, left_side=False, lower=True, t...  7.03 us
  transfers between devices with their start and end apart: 4, of which 3 were waited for; matrix products, arithmetic and copies ran while one was open for 28% of the time, Pallas kernels for 0%

commit v1 on v0

--- a/solution.py
+++ b/solution.py
@@ -58,7 +58,7 @@
     penalty = jnp.ones((), jnp.float32)
     for iteration in range(ITERS):
         partial_value = lax.dot_general(weights, basis, (((1,), (1,)), ((), ())), precision=highest)
-        predicted = lax.psum(partial_value, "feat")
+        predicted = jnp.sum(lax.all_gather(partial_value, "feat"), axis=0)
         miss, duals, residual = proximal(predicted, duals, target, penalty)
         mine = lax.dynamic_slice_in_dim(miss, offset, share, 1)
         primal_part = jnp.sum(mine * mine)

time: 299 us -> 272 us (0.910)
  waiting for transfers between devices: 97.5 us -> 69.6 us
  other arithmetic: 71.9 us -> 75.9 us
    psum x2 -> x0, waiting for transfers between devices: 45.5 us -> none  [shards(): predicted = lax.psum(partial_value, 'feat')]
    psum x2, waiting for transfers between devices: 51.9 us -> 61.3 us  [shards(): summed, primal_groups = lax.psum((local, primal_part), 'frames')]
    all_gather x0 -> x2, waiting for transfers between devices: none -> 8.18 us  [shards(): predicted = jnp.sum(lax.all_gather(partial_value, 'feat'), axis=0)]
    reduce_sum x0 -> x2, other arithmetic: none -> 4.08 us  [shards(): predicted = jnp.sum(lax.all_gather(partial_value, 'feat'), axis=0)]
  transfers between devices with their start and end apart: 4 -> 4, of which waited for: 3 -> 3; matrix products, arithmetic and copies ran while one was open for 28% -> 31% of each run, Pallas kernels for 0% -> 0%
where the time goes in v1:
time: 272 us; the launch traced here: 271 us
  other arithmetic  75.9 us (28%)
  waiting for transfers between devices  69.6 us (26%)
  blocking collectives  56.9 us (21%)
  matrix products  36.1 us (13%)
  between operations  19.3 us (7%)
  local copies, waits for them, and re-layouts  13 us (5%)
    psum x2, waiting for transfers between devices, shards(): summed, primal_groups = lax.psum((local, primal_part), 'frames')  61.3 us
    psum x2, blocking collectives, shards(): change, primal = lax.psum((jnp.sum(moved * moved), primal_groups), 'feat')  44.2 us
    another operation x6, other arithmetic, shards(): factor = jnp.linalg.cholesky(inner_matrix)  38.3 us
    another operation x4, other arithmetic, ridge_solve(): lax.linalg.triangular_solve(factor, right, left_side=False, lower=True, t...  22.8 us
    dot_general x1, matrix products, cosine_features(): jnp.dot(acoustic, projection, precision=highest, preferred_element_type=j...  13.2 us
    psum x2, blocking collectives, shards(): summed, primal_groups = lax.psum((local, primal_part), 'frames')  12.8 us
    all_gather x2, waiting for transfers between devices, shards(): predicted = jnp.sum(lax.all_gather(partial_value, 'feat'), axis=0)  8.18 us
    another operation x7, local copies, waits for them, and re-layouts, ridge_solve(): lax.linalg.triangular_solve(factor, right, left_side=False, lower=True, t...  7.02 us
  transfers between devices with their start and end apart: 4, of which 3 were waited for; matrix products, arithmetic and copies ran while one was open for 31% of the time, Pallas kernels for 0%

profile of v1, /device:TPU:0, one launch (start us, length us, event | category | flops | bytes accessed | tf_op | source)
XLA Modules:
  0.0 271.2 jit_solution(11781592948618252944)
XLA Ops:
  7.2 1.4 copy-done
  8.7 13.2 %fusion.1 = f32[256,1024]{1,0:T(8,128)S(1)} fusion(f32[256,440]{0,1:T(8,128)} %param.10, f32[440,1024]{1,0:T(8,128)S(1)} %copy-done, f32[1024]{0:T(1024)} %param.12), kind=kOutput, calls=%fused_computation.4 | convolution fusion | flops 1384644608 | bytes 3305472 | tf_op jit(solution)/shard_map/dot_general | solution.py:14
  21.8 1.9 convolution_bitcast_fusion.1
  23.7 0.2 all-reduce.6.cloned.1.call-start
  24.0 1.7 fusion.68
  25.7 1.8 copy.12
  27.5 1.1 fusion.9
  28.6 0.7 copy-done.8
  29.3 0.6 cholesky.115
  29.9 12.6 %cholesky.49 = f32[128,128]{1,0:T(8,128)S(1)} custom-call(f32[128,128]{1,0:T(8,128)} %cholesky.115), custom_call_target="Cholesky" | custom-call | tf_op jit(solution)/shard_map/jit(cholesky)/cholesky | solution.py:54
  42.5 0.6 select_reduce_fusion.1
  43.1 11.3 %custom-call.17 = f32[1,128,128]{1,2,0:T(8,128)} custom-call(f32[1,128,128]{2,1,0:T(8,128)} %get-tuple-element.63), custom_call_target="InvertDiagBlocksLowerTriangular" | custom-call | tf_op jit(solution)/shard_map/jit(cholesky)/cholesky | solution.py:54
  54.4 0.7 cholesky.111
  55.1 1.7 constant_dynamic-update-slice_fusion
  56.8 1.7 convolution_subtract_fusion.6
  58.6 12.5 %cholesky.103 = f32[128,128]{1,0:T(8,128)S(1)} custom-call(f32[128,128]{1,0:T(8,128)} %convolution_subtract_fusion.6), custom_call_target="Cholesky" | custom-call | tf_op jit(solution)/shard_map/jit(cholesky)/cholesky | solution.py:54
  71.1 0.6 select_reduce_fusion
  71.7 0.6 compare_reduce_fusion
  73.6 1.7 select_select_fusion
  75.3 0.1 broadcast.169
  75.4 7.0 %while.8 = (s32[]{:T(128)}, f32[256,256]{1,0:T(8,128)}, s32[2,2]{1,0:T(2,128)S(1)}, f32[2,128,128]{2,1,0:T(8,128)}, s32[]{:T(128)}) while((s32[]{:T(128)}, f32[256,256]{1,0:T(8,128)}, s32[2,2]{1,0:T(2,128)S(1)}, f32[2,128,128]{2,1,0:T(8,128)}, s32[]{:T(128)}) %tuple.44), condition=%wide.while_cond, body=%wide.while_body.sunk | while | flops 2 | bytes 132205 | solution.py:21
  75.4 0.6 fusion.99
  76.0 2.9 %bitcast_dynamic-update-slice_fusion.2 = f32[2,128,128]{2,1,0:T(8,128)} fusion(f32[2,128,128]{2,1,0:T(8,128)} %get-tuple-element.105, s32[]{:T(128)S(6)} %copy.19, f32[256,256]{1,0:T(8,128)} %get-tuple-element.108, s32[]{:T(128)} %bitcast.87, s32[]{:T(128)} %bitcast.88), kind=kLoop, calls=%fused_computation.clone.1 | loop fusion | bytes 132100 | tf_op jit(solution)/shard_map/triangular_solve | solution.py:21
  78.9 0.6 fusion.99
  79.5 2.8 %bitcast_dynamic-update-slice_fusion.2 = f32[2,128,128]{2,1,0:T(8,128)} fusion(f32[2,128,128]{2,1,0:T(8,128)} %get-tuple-element.105, s32[]{:T(128)S(6)} %copy.19, f32[256,256]{1,0:T(8,128)} %get-tuple-element.108, s32[]{:T(128)} %bitcast.87, s32[]{:T(128)} %bitcast.88), kind=kLoop, calls=%fused_computation.clone.1 | loop fusion | bytes 132100 | tf_op jit(solution)/shard_map/triangular_solve | solution.py:21
  82.3 21.1 %custom-call.20 = f32[2,128,128]{1,2,0:T(8,128)} custom-call(f32[2,128,128]{2,1,0:T(8,128)} %get-tuple-element.33), custom_call_target="InvertDiagBlocksLowerTriangular" | custom-call | tf_op jit(solution)/shard_map/triangular_solve/custom-call.0 | solution.py:21
  103.4 2.0 reduce_sum.54
  105.5 1.7 fusion.65
  107.2 1.9 convolution_multiply_fusion.1
  109.1 1.2 fusion.69
  110.3 0.3 fusion.32
  110.6 0.3 convolution_subtract_fusion.5
  110.9 0.3 fusion.46
  111.2 0.3 fusion.47
  111.5 0.3 convolution_subtract_fusion.4
  111.8 0.3 fusion.43
  112.1 1.6 fusion.3
  113.7 0.0 all-gather.9.cloned.1.call-start
  113.8 36.7 %all-reduce.6.cloned.1.call-done = f32[147,1024]{1,0:T(8,128)} async-done(((f32[147,1024]{1,0:T(8,128)}), f32[147,1024]{1,0:T(8,128)}) %all-reduce.6.cloned.1.call-update) | async-done | bytes 602128 | tf_op jit(solution)/shard_map/psum | solution.py:73
  150.5 3.0 %convolution_bitcast_fusion = f32[1,147,256]{2,1,0:T(8,128)} fusion(f32[256,1024]{1,0:T(8,128)S(1)} %fusion.1, f32[147,1024]{1,0:T(8,128)} %all-reduce.6.cloned.1.call-done), kind=kOutput, calls=%fused_computation.13 | convolution fusion | flops 462572544 | bytes 1801216 | tf_op jit(solution)/shard_map/dot_general | solution.py:60
  153.5 0.0 all-reduce.8.cloned.1.call-start
  153.6 1.6 multiply_reduce_fusion.3
  155.2 6.4 %psum.56 = f32[]{:T(128)} all-reduce(f32[]{:T(128)} %multiply_reduce_fusion.3), channel_id=1, replica_groups=mesh['frames'=4,'feat'=8] {'frames'}, use_global_device_ids=true, to_apply=%region_2.3 | all-reduce | flops 1 | bytes 8 | tf_op jit(solution)/shard_map/psum | solution.py:73
  161.5 1.9 multiply_reduce_fusion.1
  163.4 22.2 %all-reduce.2 = (f32[]{:T(128)}, f32[]{:T(128)}) all-reduce(f32[]{:T(128)} %psum.56, f32[]{:T(128)} %multiply_reduce_fusion.1), channel_id=1, replica_groups=mesh['frames'=4,'feat'=8] {'feat'}, use_global_device_ids=true, to_apply=%region_3.4 | all-reduce | flops 2 | bytes 16 | tf_op jit(solution)/shard_map/psum | solution.py:76
  187.1 8.2 %all-gather.9.cloned.1.call-done = f32[8,147,256]{2,1,0:T(8,128)} async-done(((f32[1,147,256]{2,1,0:T(8,128)}), f32[8,147,256]{2,1,0:T(8,128)}) %all-gather.9.cloned.1.call-update) | async-done | bytes 1204240 | tf_op jit(solution)/shard_map/all_gather | solution.py:61
  195.2 2.0 reduce_sum.57
  197.3 1.9 convolution_multiply_fusion
  199.2 1.2 fusion.70
  200.4 0.3 fusion.30
  200.7 0.3 convolution_subtract_fusion.3
  201.0 0.3 fusion.44
  201.3 0.3 fusion.45
  201.6 0.3 convolution_subtract_fusion.2
  201.9 0.3 fusion.42
  202.2 1.6 fusion.5
  203.9 1.1 fusion.53
  204.9 0.7 multiply_reduce_fusion.2
  205.7 6.4 %psum.61 = f32[]{:T(128)} all-reduce(f32[]{:T(128)} %multiply_reduce_fusion.2), channel_id=1, replica_groups=mesh['frames'=4,'feat'=8] {'frames'}, use_global_device_ids=true, to_apply=%region_14.17 | all-reduce | flops 1 | bytes 8 | tf_op jit(solution)/shard_map/psum | solution.py:73
  212.1 24.6 %all-reduce.8.cloned.1.call-done = f32[147,1024]{1,0:T(8,128)} async-done(((f32[147,1024]{1,0:T(8,128)}), f32[147,1024]{1,0:T(8,128)}) %all-reduce.8.cloned.1.call-update) | async-done | bytes 602128 | tf_op jit(solution)/shard_map/psum | solution.py:73
  236.7 2.6 multiply_reduce_fusion
  239.3 22.0 %all-reduce.1 = (f32[]{:T(128)}, f32[]{:T(128)}) all-reduce(f32[]{:T(128)} %psum.61, f32[]{:T(128)} %get-tuple-element.52), channel_id=1, replica_groups=mesh['frames'=4,'feat'=8] {'feat'}, use_global_device_ids=true, to_apply=%region_15.18 | all-reduce | flops 2 | bytes 16 | tf_op jit(solution)/shard_map/psum | solution.py:76
  262.8 0.1 dynamic-slice_multiply_fusion
  262.9 0.7 copy.13
  (28 shorter events, 0.2 us)
Async XLA Ops:
  7.2 1.5 copy-start
  7.2 14.7 %copy-start.2 = (f32[147,1024]{1,0:T(8,128)S(1)}, f32[147,1024]{1,0:T(8,128)}, u32[]{:S(2)}) copy-start(f32[147,1024]{1,0:T(8,128)} %param.14) | copy-start | bytes 1806340
  7.2 96.2 %all-gather.7.cloned.1.call-start = ((), (), s32[]{:S(2)}) async-start(), calls=%async_computation.2 | async-start | bytes 1400832 | tf_op jit(solution)/shard_map/all_gather | solution.py:61
  23.7 126.8 %all-reduce.6.cloned.1.call-start = ((), (), s32[]{:S(2)}) async-start(), calls=%async_computation | async-start | bytes 1245184 | tf_op jit(solution)/shard_map/psum | solution.py:73
  28.6 0.7 copy-start.8
  55.1 50.4 %copy-start.9 = (s32[256]{0:T(256)S(1)}, s32[256]{0:T(256)}, u32[]{:S(2)}) copy-start(s32[256]{0:T(256)} %param.13) | copy-start | bytes 3076
  107.2 3.1 %copy-start.5 = (f32[147,256]{1,0:T(8,128)}, f32[147,256]{1,0:T(8,128)S(1)}, u32[]{:S(2)}) copy-start(f32[147,256]{1,0:T(8,128)S(1)} %get-tuple-element.54) | copy-start | bytes 451588
  107.2 3.1 %copy-start.6 = (f32[2,128,128]{1,2,0:T(8,128)S(1)}, f32[2,128,128]{1,2,0:T(8,128)}, u32[]{:S(2)}) copy-start(f32[2,128,128]{1,2,0:T(8,128)} %custom-call.20) | copy-start | bytes 393220
  107.2 3.4 %copy-start.3 = (f32[256,256]{1,0:T(8,128)S(1)}, f32[256,256]{1,0:T(8,128)}, u32[]{:S(2)}) copy-start(f32[256,256]{1,0:T(8,128)} %get-tuple-element.117) | copy-start | bytes 786436
  113.7 81.5 %all-gather.9.cloned.1.call-start = ((), (), s32[]{:S(2)}) async-start(), calls=%async_computation.3 | async-start | bytes 1400832 | tf_op jit(solution)/shard_map/all_gather | solution.py:61
  150.5 11.1 %copy-start.1 = (f32[147,1024]{1,0:T(8,128)S(1)}, f32[147,1024]{1,0:T(8,128)}, u32[]{:S(2)}) copy-start(f32[147,1024]{1,0:T(8,128)} %all-reduce.6.cloned.1.call-done) | copy-start | bytes 1806340
  153.5 83.2 %all-reduce.8.cloned.1.call-start = ((), (), s32[]{:S(2)}) async-start(), calls=%async_computation.1 | async-start | bytes 1245184 | tf_op jit(solution)/shard_map/psum | solution.py:73
  197.3 3.1 %copy-start.7 = (f32[2,128,128]{1,2,0:T(8,128)S(1)}, f32[2,128,128]{1,2,0:T(8,128)}, u32[]{:S(2)}) copy-start(f32[2,128,128]{1,2,0:T(8,128)} %custom-call.20) | copy-start | bytes 393220
  197.3 3.4 %copy-start.4 = (f32[256,256]{1,0:T(8,128)S(1)}, f32[256,256]{1,0:T(8,128)}, u32[]{:S(2)}) copy-start(f32[256,256]{1,0:T(8,128)} %get-tuple-element.117) | copy-start | bytes 786436
Sparse Core Ops, SparseCore 0:
  23.8 45.1 all-gather.6
  113.8 36.5 all-reduce.5
  153.7 41.5 all-gather.8
  204.0 32.6 all-reduce.7
